TPU v7x, 32 devices: a whole 2x2x4 slice. The times are simulated.
32 devices in a mesh: nodes: 8 (over y, x, core), cols: 4 (over z).
Axes of the slice: x: 2, y: 2, z: 4, core: 2. Of those that a mesh axis runs over, the one named last changes fastest.
Arguments:
- features: bfloat16 [1024, 512], P('nodes', 'cols'), may hold values from -6 to 6
- weight: bfloat16 [512, 512], P(None, 'cols'), may hold values from -0.25 to 0.25
- degree: int32 [1024], P('nodes'), may hold values from 1 to 64
- tile_cols: int32 [8, 8], P('nodes'), may hold values from 0 to 7, as said below
- tile_count: int32 [8], P('nodes'), may hold values from 1 to 8, as said below
- tile_codes: int32 [8, 8], P('nodes'), may hold values from 0 to 1048575
- cotangent: bfloat16 [1024, 512], P('nodes', 'cols'), may hold values from -6 to 6
Outputs:
- activation: bfloat16 [1024, 512], P('nodes', 'cols')
- weight_grad: float32 [512, 512], P(None, 'cols')
- feats_grad: float32 [1024, 512], P('nodes', 'cols')
Inputs may be any that keep to these rules, and one draw needn't show every extreme that they name: `tile_cols`: each row lists every node block once, and row i begins with block i. The tiles of row block i are those of its first tile_count[i] slots; some row block holds all 8.
All inputs are finite; a program needn't handle non-finite values.
Results may differ from a plain program's by a relative error of at most 0.0065.
Values may be sent and summed in bfloat16 or wider, within the bound.
A program may use at most 64 MiB of HBM per device.

v0:
```python
import jax
import jax.numpy as jnp
from jax import lax
from jax.sharding import PartitionSpec as P

TILE = 128


def tile_bits(pattern_code):
    line_ids = jnp.arange(TILE, dtype=jnp.int32)
    hashed = (
        pattern_code[..., None, None] * 73856093
        ^ line_ids[:, None] * 19349663
        ^ line_ids[None, :] * 83492791
    )
    hashed = hashed ^ hashed >> 13
    hashed = hashed * 1274126177
    hashed = hashed ^ hashed >> 16
    return hashed & 63 == 0


def make_tiles(matches, code_table, live_limit, own, identity):
    slot_ids = jnp.arange(matches.shape[1], dtype=jnp.int32)
    slot_index = jnp.sum(jnp.where(matches, slot_ids[None, :], 0), axis=1, dtype=jnp.int32)
    code_value = jnp.sum(jnp.where(matches, code_table, 0), axis=1, dtype=jnp.int32)
    pattern = tile_bits(code_value) & (slot_index < live_limit)[:, None, None]
    values = (
        pattern.astype(jnp.float32)
        + jnp.where(own, 1.0, 0.0).astype(jnp.float32)[:, None, None] * identity
    )
    return values.astype(jnp.bfloat16)


def body(features, weight, degree, tile_cols, tile_count, tile_codes, cotangent):
    my_block = lax.axis_index("nodes")
    identity = jnp.eye(TILE, dtype=jnp.float32)
    inv_root = lax.rsqrt(degree.astype(jnp.float32))[:, None]
    scaled = (features.astype(jnp.float32) * inv_root).astype(jnp.bfloat16)
    my_cols = tile_cols[0]
    my_codes = tile_codes[0]
    my_count = tile_count[0]
    pieces = lax.all_gather(scaled[None], "nodes", axis=0, tiled=True)
    count_blocks = pieces.shape[0]
    targets = jnp.arange(count_blocks, dtype=jnp.int32)
    matches = targets[:, None] == my_cols[None, :]
    tiles = make_tiles(matches, my_codes[None, :], my_count, targets == my_block, identity)
    gathered = lax.dot_general(
        tiles, pieces, (((0, 2), (0, 1)), ((), ())), preferred_element_type=jnp.float32
    )
    aggregated = (inv_root * gathered).astype(jnp.bfloat16)
    agg_full = lax.all_gather(aggregated, "cols", axis=1, tiled=True)
    pre = jnp.dot(agg_full, weight, preferred_element_type=jnp.float32)
    activation = jax.nn.silu(pre).astype(jnp.bfloat16)
    sigma = jax.nn.sigmoid(pre)
    grad_pre = (cotangent.astype(jnp.float32) * sigma * (1.0 + pre * (1.0 - sigma))).astype(
        jnp.bfloat16
    )
    partial_grad = lax.dot_general(
        agg_full, grad_pre, (((0,), (0,)), ((), ())), preferred_element_type=jnp.float32
    )
    weight_grad = lax.psum(partial_grad, "nodes")
    terms = lax.dot_general(
        grad_pre, weight, (((1,), (1,)), ((), ())), preferred_element_type=jnp.float32
    )
    grad_agg = lax.psum_scatter(terms, "cols", scatter_dimension=1, tiled=True)
    grad_scaled = (inv_root * grad_agg).astype(jnp.bfloat16)
    all_cols, all_counts, all_codes = (
        lax.all_gather(tile_cols, "nodes", axis=0, tiled=True),
        lax.all_gather(tile_count, "nodes", axis=0, tiled=True),
        lax.all_gather(tile_codes, "nodes", axis=0, tiled=True),
    )
    pieces = lax.all_gather(grad_scaled[None], "nodes", axis=0, tiled=True)
    count_blocks = pieces.shape[0]
    row_ids = jnp.arange(count_blocks, dtype=jnp.int32)
    tiles = make_tiles(all_cols == my_block, all_codes, all_counts, row_ids == my_block, identity)
    back_total = lax.dot_general(
        tiles, pieces, (((0, 1), (0, 1)), ((), ())), preferred_element_type=jnp.float32
    )
    feats_grad = inv_root * back_total
    return (activation, weight_grad, feats_grad)


def solution(mesh):
    in_specs = (
        P("nodes", "cols"),
        P(None, "cols"),
        P("nodes"),
        P("nodes", None),
        P("nodes"),
        P("nodes", None),
        P("nodes", "cols"),
    )
    out_specs = (P("nodes", "cols"), P(None, "cols"), P("nodes", "cols"))
    return jax.shard_map(body, mesh=mesh, in_specs=in_specs, out_specs=out_specs, check_vma=False)
```

profile of v0, /device:TPU:0, one launch (start us, length us, event | category | flops | bytes accessed | tf_op | source)
XLA Modules:
  0.0 118.2 jit_solution(6654077568115102820)
XLA Ops:
  8.0 0.0 copy-start
  8.0 0.0 reduce-scatter.2.cloned.1.call-start
  8.1 0.0 copy-start.2
  8.1 0.0 copy-start.4
  8.1 0.6 copy-done.4
  8.8 10.2 %all-gather.2 = s32[8,1,8]{2,1,0:T(1,128)S(1)} all-gather(s32[1,1,8]{2,1,0:T(1,128)S(1)} %bitcast.36), channel_id=1, replica_groups=mesh['nodes'=8,'cols'=4] {'nodes'}, dimensions={0}, use_global_device_ids=true | all-gather | bytes 288 | tf_op jit(solution)/shard_map/all_gather | solution.py:68
  19.0 0.0 copy-start.3
  19.0 0.7 copy-done.3
  19.6 0.0 copy-start.5
  19.6 8.8 %all-gather.3 = s32[8,1,8]{2,1,0:T(1,128)S(1)} all-gather(s32[1,1,8]{2,1,0:T(1,128)S(1)} %bitcast.34), channel_id=1, replica_groups=mesh['nodes'=8,'cols'=4] {'nodes'}, dimensions={0}, use_global_device_ids=true | all-gather | bytes 288 | tf_op jit(solution)/shard_map/all_gather | solution.py:70
  28.5 0.0 copy-done.5
  28.5 0.0 copy-done.2
  28.5 0.1 multiply_convert_fusion.3
  28.6 8.3 %all-gather = bf16[1024,128]{1,0:T(8,128)(2,1)S(1)} all-gather(bf16[128,128]{1,0:T(8,128)(2,1)S(1)} %multiply_convert_fusion.3), channel_id=2, replica_groups=mesh['nodes'=8,'cols'=4] {'nodes'}, dimensions={0}, use_global_device_ids=true | all-gather | bytes 294912 | tf_op jit(solution)/shard_map/all_gather | solution.py:42
  37.6 0.1 select_reduce_fusion
  37.7 0.2 select_reduce_fusion.2
  37.9 0.1 broadcast_xor_fusion
  38.0 0.5 fusion.2
  38.5 12.5 %all_gather.19 = bf16[128,512]{1,0:T(8,128)(2,1)S(1)} all-gather(bf16[128,128]{1,0:T(8,128)(2,1)S(1)} %fusion.2), channel_id=1, replica_groups=mesh['nodes'=8,'cols'=4] {'cols'}, dimensions={1}, use_global_device_ids=true | all-gather | bytes 163840 | tf_op jit(solution)/shard_map/all_gather | solution.py:51
  50.9 0.0 copy-done
  51.0 0.0 copy-start.1
  51.0 0.8 multiply_convert_fusion.2
  51.8 0.0 copy-done.1
  51.8 0.9 fusion.46
  52.7 0.0 reduce-scatter.2.cloned.1.call-update
  52.7 0.0 all-reduce.3.cloned.1.call-start
  52.7 0.0 copy-start.6
  52.8 0.6 copy-done.6
  53.4 0.6 dynamic-slice
  54.0 0.8 dynamic-update-slice
  54.7 0.9 fusion.47
  55.7 0.0 all-reduce.3.cloned.1.call-update
  55.7 7.4 %all-reduce = s32[8]{0:T(128)S(1)} all-reduce(s32[8]{0:T(128)S(1)} %dynamic-update-slice), channel_id=1, replica_groups=mesh['nodes'=8,'cols'=4] {'nodes'}, use_global_device_ids=true, to_apply=%add | all-reduce | flops 8 | bytes 64
  63.1 8.6 %reduce-scatter.2.cloned.1.call-done = f32[128,128]{1,0:T(8,128)} async-done(((f32[128,512]{1,0:T(8,128)}), f32[128,128]{1,0:T(8,128)}) %reduce-scatter.2.cloned.1.call-update) | async-done | bytes 65552 | tf_op jit(solution)/shard_map/reduce_scatter | solution.py:65
  71.7 0.9 multiply_convert_fusion
  72.6 9.5 %all-gather.1 = bf16[1024,128]{1,0:T(8,128)(2,1)S(1)} all-gather(bf16[128,128]{1,0:T(8,128)(2,1)S(1)} %multiply_convert_fusion), channel_id=3, replica_groups=mesh['nodes'=8,'cols'=4] {'nodes'}, dimensions={0}, use_global_device_ids=true | all-gather | bytes 294912 | tf_op jit(solution)/shard_map/all_gather | solution.py:72
  82.1 1.1 fusion
  83.1 26.0 %all-reduce.3.cloned.1.call-done = f32[512,128]{1,0:T(8,128)} async-done(((f32[512,128]{1,0:T(8,128)}), f32[512,128]{1,0:T(8,128)}) %all-reduce.3.cloned.1.call-update) | async-done | bytes 262160 | tf_op jit(solution)/shard_map/psum | solution.py:61
  109.1 1.7 %copy.18 = f32[512,128]{1,0:T(8,128)} copy(f32[512,128]{1,0:T(8,128)} %all-reduce.3.cloned.1.call-done) | data formatting | bytes 524288
  (9 shorter events, 0.0 us)
Async XLA Ops:
  8.0 43.0 %copy-start = (bf16[512,128]{1,0:T(8,128)(2,1)S(1)}, bf16[512,128]{1,0:T(8,128)(2,1)}, u32[]{:S(2)}) copy-start(bf16[512,128]{1,0:T(8,128)(2,1)} %param.8) | copy-start | bytes 393220
  8.0 63.7 %reduce-scatter.2.cloned.1.call-start = ((), (), s32[]{:S(2)}) async-start(), calls=%async_computation.2 | async-start | bytes 327680 | tf_op jit(solution)/shard_map/reduce_scatter | solution.py:65
  8.1 20.4 %copy-start.2 = (bf16[128,128]{1,0:T(8,128)(2,1)S(1)}, bf16[128,128]{1,0:T(8,128)(2,1)}, u32[]{:S(2)}) copy-start(bf16[128,128]{1,0:T(8,128)(2,1)} %param.7) | copy-start | bytes 98308
  8.1 0.7 copy-start.4
  19.0 0.7 copy-start.3
  19.6 8.8 %copy-start.5 = (s32[128]{0:T(128)S(1)}, s32[128]{0:T(128)}, u32[]{:S(2)}) copy-start(s32[128]{0:T(128)} %param.9) | copy-start | bytes 1540
  51.0 0.8 copy-start.1
  52.7 56.4 %all-reduce.3.cloned.1.call-start = ((), (), s32[]{:S(2)}) async-start(), calls=%async_computation.1 | async-start | bytes 524288 | tf_op jit(solution)/shard_map/psum | solution.py:61
  52.7 0.7 copy-start.6
Sparse Core Ops, SparseCore 0:
  52.8 18.8 reduce-scatter.1
Sparse Core Ops, SparseCore 1:
  56.8 52.3 all-reduce.2
where the time goes:
time: 119 us; the launch traced here: 118 us
  blocking collectives  56.7 us (48%)
  waiting for transfers between devices  34.7 us (29%)
  between operations  16.2 us (14%)
  local copies, waits for them, and re-layouts  4.98 us (4%)
  matrix products  4.16 us (3%)
  other arithmetic  1.41 us (1%)
    psum x1, waiting for transfers between devices, body(): weight_grad = lax.psum(partial_grad, 'nodes')  26 us
    all_gather x1, blocking collectives, body(): agg_full = lax.all_gather(aggregated, 'cols', axis=1, tiled=True)  12.5 us
    all_gather x1, blocking collectives, body(): lax.all_gather(tile_cols, 'nodes', axis=0, tiled=True)  10.2 us
    all_gather x1, blocking collectives, body(): pieces = lax.all_gather(grad_scaled[None], 'nodes', axis=0, tiled=True)  9.48 us
    all_gather x1, blocking collectives, body(): lax.all_gather(tile_codes, 'nodes', axis=0, tiled=True)  8.84 us
    reduce_scatter x1, waiting for transfers between devices, body(): grad_agg = lax.psum_scatter(terms, 'cols', scatter_dimension=1, tiled=True)  8.63 us
    all_gather x1, blocking collectives, body(): pieces = lax.all_gather(scaled[None], 'nodes', axis=0, tiled=True)  8.34 us
    unnamed x1, blocking collectives  7.36 us
  transfers between devices with their start and end apart: 2, of which 2 were waited for; matrix products, arithmetic and copies ran while one was open for 4% of the time, Pallas kernels for 0%

commit v1 on v0

--- a/solution.py
+++ b/solution.py
@@ -58,7 +58,7 @@
     partial_grad = lax.dot_general(
         agg_full, grad_pre, (((0,), (0,)), ((), ())), preferred_element_type=jnp.float32
     )
-    weight_grad = lax.psum(partial_grad, "nodes")
+    weight_grad = jnp.sum(lax.all_gather(partial_grad, "nodes"), axis=0)
     terms = lax.dot_general(
         grad_pre, weight, (((1,), (1,)), ((), ())), preferred_element_type=jnp.float32
     )

time: 119 us -> 94.8 us (0.80)
  waiting for transfers between devices: 34.7 us -> 9.26 us
  other arithmetic: 1.41 us -> 5.92 us
  local copies, waits for them, and re-layouts: 4.98 us -> 1.46 us
    psum x1 -> x0, waiting for transfers between devices: 26 us -> none  [body(): weight_grad = lax.psum(partial_grad, 'nodes')]
    unnamed x18 -> x9, local copies, waits for them, and re-layouts: 4.98 us -> 1.46 us
    reduce_sum x0 -> x1, other arithmetic: none -> 2.42 us  [body(): weight_grad = jnp.sum(lax.all_gather(partial_grad, 'nodes'), axis=0)]
    all_gather x1, blocking collectives: 10.2 us -> 8.6 us  [body(): lax.all_gather(tile_cols, 'nodes', axis=0, tiled=True)]
    all_gather x1, blocking collectives: 8.84 us -> 10.3 us  [body(): lax.all_gather(tile_codes, 'nodes', axis=0, tiled=True)]
  transfers between devices with their start and end apart: 2 -> 2, of which waited for: 2 -> 1; matrix products, arithmetic and copies ran while one was open for 4% -> 5% of each run, Pallas kernels for 0% -> 0%
where the time goes in v1:
time: 94.8 us; the launch traced here: 94.4 us
  blocking collectives  57.3 us (60%)
  between operations  16.2 us (17%)
  waiting for transfers between devices  9.26 us (10%)
  other arithmetic  5.92 us (6%)
  matrix products  4.19 us (4%)
  local copies, waits for them, and re-layouts  1.46 us (2%)
    all_gather x1, blocking collectives, body(): agg_full = lax.all_gather(aggregated, 'cols', axis=1, tiled=True)  12.5 us
    all_gather x1, blocking collectives, body(): lax.all_gather(tile_codes, 'nodes', axis=0, tiled=True)  10.3 us
    all_gather x1, blocking collectives, body(): pieces = lax.all_gather(grad_scaled[None], 'nodes', axis=0, tiled=True)  10.2 us
    reduce_scatter x1, waiting for transfers between devices, body(): grad_agg = lax.psum_scatter(terms, 'cols', scatter_dimension=1, tiled=True)  9.22 us
    all_gather x1, blocking collectives, body(): lax.all_gather(tile_cols, 'nodes', axis=0, tiled=True)  8.6 us
    all_gather x1, blocking collectives, body(): pieces = lax.all_gather(scaled[None], 'nodes', axis=0, tiled=True)  8.45 us
    unnamed x1, blocking collectives  7.24 us
    reduce_sum x1, other arithmetic, body(): weight_grad = jnp.sum(lax.all_gather(partial_grad, 'nodes'), axis=0)  2.42 us
  transfers between devices with their start and end apart: 2, of which 1 were waited for; matrix products, arithmetic and copies ran while one was open for 5% of the time, Pallas kernels for 0%

profile of v1, /device:TPU:0, one launch (start us, length us, event | category | flops | bytes accessed | tf_op | source)
XLA Modules:
  0.0 94.4 jit_solution(12111465652870028881)
XLA Ops:
  8.0 0.0 copy-start
  8.0 0.0 copy-start.1
  8.0 0.0 reduce-scatter.2.cloned.1.call-start
  8.1 10.3 %all-gather.4 = s32[8,1,8]{2,1,0:T(1,128)S(1)} all-gather(s32[1,1,8]{2,1,0:T(1,128)} %bitcast.36), channel_id=1, replica_groups=mesh['nodes'=8,'cols'=4] {'nodes'}, dimensions={0}, use_global_device_ids=true | all-gather | bytes 288 | tf_op jit(solution)/shard_map/all_gather | solution.py:70
  18.4 8.6 %all-gather.3 = s32[8,1,8]{2,1,0:T(1,128)S(1)} all-gather(s32[1,1,8]{2,1,0:T(1,128)} %bitcast.38), channel_id=1, replica_groups=mesh['nodes'=8,'cols'=4] {'nodes'}, dimensions={0}, use_global_device_ids=true | all-gather | bytes 288 | tf_op jit(solution)/shard_map/all_gather | solution.py:68
  27.0 0.7 convert_rsqrt_fusion
  27.7 0.8 multiply_convert_fusion.3
  28.5 0.0 copy-start.2
  28.6 8.4 %all-gather = bf16[1024,128]{1,0:T(8,128)(2,1)S(1)} all-gather(bf16[128,128]{1,0:T(8,128)(2,1)S(1)} %multiply_convert_fusion.3), channel_id=2, replica_groups=mesh['nodes'=8,'cols'=4] {'nodes'}, dimensions={0}, use_global_device_ids=true | all-gather | bytes 294912 | tf_op jit(solution)/shard_map/all_gather | solution.py:42
  37.7 0.1 select_reduce_fusion
  37.8 0.8 select_reduce_fusion.2
  38.6 0.1 broadcast_xor_fusion
  38.7 0.5 fusion.2
  39.2 12.5 %all_gather.25 = bf16[128,512]{1,0:T(8,128)(2,1)S(1)} all-gather(bf16[128,128]{1,0:T(8,128)(2,1)S(1)} %fusion.2), channel_id=1, replica_groups=mesh['nodes'=8,'cols'=4] {'cols'}, dimensions={1}, use_global_device_ids=true | all-gather | bytes 163840 | tf_op jit(solution)/shard_map/all_gather | solution.py:51
  51.7 0.0 copy-done
  51.7 0.8 multiply_convert_fusion.2
  52.5 0.0 copy-done.1
  52.5 0.9 fusion.46
  53.4 0.0 reduce-scatter.2.cloned.1.call-update
  53.5 0.0 all-gather.7.cloned.1.call-start
  53.5 0.9 fusion.47
  54.4 0.0 all-gather.7.cloned.1.call-update
  54.5 0.0 copy-done.2
  54.5 0.7 dynamic-slice
  55.1 0.8 dynamic-update-slice
  55.9 7.2 %all-reduce = s32[8]{0:T(128)S(1)} all-reduce(s32[8]{0:T(128)S(1)} %dynamic-update-slice), channel_id=1, replica_groups=mesh['nodes'=8,'cols'=4] {'nodes'}, use_global_device_ids=true, to_apply=%add | all-reduce | flops 8 | bytes 64
  63.2 9.2 %reduce-scatter.2.cloned.1.call-done = f32[128,128]{1,0:T(8,128)} async-done(((f32[128,512]{1,0:T(8,128)}), f32[128,128]{1,0:T(8,128)}) %reduce-scatter.2.cloned.1.call-update) | async-done | bytes 65552 | tf_op jit(solution)/shard_map/reduce_scatter | solution.py:65
  72.4 0.9 multiply_convert_fusion
  73.3 10.2 %all-gather.2 = bf16[1024,128]{1,0:T(8,128)(2,1)S(1)} all-gather(bf16[128,128]{1,0:T(8,128)(2,1)S(1)} %multiply_convert_fusion), channel_id=4, replica_groups=mesh['nodes'=8,'cols'=4] {'nodes'}, dimensions={0}, use_global_device_ids=true | all-gather | bytes 294912 | tf_op jit(solution)/shard_map/all_gather | solution.py:72
  83.5 1.1 %fusion = f32[128,128]{1,0:T(8,128)} fusion(bf16[8,128,128]{2,1,0:T(8,128)(2,1)S(1)} %bitcast.33, s32[8,128]{1,0:T(8,128)S(1)} %get-tuple-element.7, f32[128,128]{0,1:T(8,128)S(1)} %fusion.35, f32[8]{0:T(128)S(1)} %compare_select_fusion, s32[128]{0:T(128)S(1)} %iota_multiply_fusion, pred[8]{0:T(512)(128)(4,1)S(1)} %lt.15, f32[128]{0:T(128)S(1)} %convert_rsqrt_fusion), kind=kOutput, calls=%fused_computation.1 | convolution fusion | flops 35274752 | bytes 398376 | tf_op jit(solution)/shard_map/dot_general | solution.py:76
  84.5 0.0 all-gather.7.cloned.1.call-done
  84.5 2.4 %reduce_sum.47 = f32[512,128]{1,0:T(8,128)} reduce(f32[8,512,128]{2,1,0:T(8,128)} %bitcast.31, f32[]{:T(128)} %constant.11.clone.1), dimensions={0}, to_apply=%region_2.3 | reduce | flops 458752 | bytes 2359300 | tf_op jit(solution)/shard_map/reduce_sum | solution.py:61
  (8 shorter events, 0.0 us)
Async XLA Ops:
  8.0 43.7 %copy-start = (bf16[512,128]{1,0:T(8,128)(2,1)S(1)}, bf16[512,128]{1,0:T(8,128)(2,1)}, u32[]{:S(2)}) copy-start(bf16[512,128]{1,0:T(8,128)(2,1)} %param.8) | copy-start | bytes 393220
  8.0 44.5 %copy-start.1 = (bf16[128,128]{1,0:T(8,128)(2,1)S(1)}, bf16[128,128]{1,0:T(8,128)(2,1)}, u32[]{:S(2)}) copy-start(bf16[128,128]{1,0:T(8,128)(2,1)} %param.13) | copy-start | bytes 98308
  8.0 64.4 %reduce-scatter.2.cloned.1.call-start = ((), (), s32[]{:S(2)}) async-start(), calls=%async_computation.1 | async-start | bytes 327680 | tf_op jit(solution)/shard_map/reduce_scatter | solution.py:65
  28.5 25.9 %copy-start.2 = (u32[32]{0:T(128)S(1)}, u32[32]{0:T(128)}, u32[]{:S(2)}) copy-start(u32[32]{0:T(128)} %constant.35) | copy-start | bytes 388
  53.5 31.1 %all-gather.7.cloned.1.call-start = ((), (), s32[]{:S(2)}) async-start(), calls=%async_computation.2 | async-start | bytes 2359296 | tf_op jit(solution)/shard_map/all_gather | solution.py:61
Sparse Core Ops, SparseCore 0:
  53.6 18.7 reduce-scatter.1
Sparse Core Ops, SparseCore 1:
  56.4 27.9 all-gather.6
